TPU v7x, 256 devices: a whole 4x4x8 slice. The times are simulated.
256 devices in a mesh: ent: 64 (over z, y, core), rel: 4 (over x).
Axes of the slice: x: 4, y: 4, z: 8, core: 2. Of those that a mesh axis runs over, the one named last changes fastest.
Arguments:
- entity_rows: bfloat16 [65536, 256], P('ent'), may hold values from -2.5 to 2.5
- request_rows: int32 [64, 64, 32], P('ent'), may hold values from 0 to 1023
- edge_heads: int32 [262144], P(('ent', 'rel')), may hold values from 0 to 1023
- edge_rels: int32 [262144], P(('ent', 'rel')), may hold values from 0 to 7
- edge_tails: int32 [262144], P(('ent', 'rel')), may hold values from 0 to 2047
- edge_counts: int32 [256], P(('ent', 'rel')), may hold values from 1 to 1024, 163840 in all
- negative_rows: int32 [65536], P(('ent', 'rel')), may hold values from 0 to 1023
- relation_blocks: bfloat16 [32, 8, 32, 32], P('rel'), may hold values from -1 to 1
Outputs:
- entity_grad: float32 [65536, 256], P('ent')
- relation_grad: float32 [32, 8, 32, 32], P('rel')
Inputs may be any that keep to these rules, and one draw needn't show every extreme that they name: Edge slots of bucket b at or past edge_counts[b] are ignored; some bucket is full in every draw.
All inputs are finite; a program needn't handle non-finite values. No bound on the sum of `edge_counts` on one device may be relied on, other than what follows from the above.
Results may differ from a plain program's by a relative error of at most 0.009.
Values may be sent and summed in bfloat16 or wider, within the bound.
No kernel may reach another device: no remote copies, remote signals or barrier semaphores. Data moves between devices by JAX's collectives and lax.ppermute only.
A program may use at most 64 MiB of HBM per device.

v0:
```python
import math
import jax
import jax.numpy as jnp
from jax import lax
from jax.sharding import PartitionSpec as P


def pick_rows(indices, source_table):
    row_total = indices.shape[0]
    block_size = math.gcd(row_total, 256)
    grouped = indices.reshape(row_total // block_size, block_size)
    columns = jnp.arange(source_table.shape[0], dtype=jnp.int32)

    def pick_block(index_block):
        one_hot = (index_block[:, None] == columns[None, :]).astype(jnp.bfloat16)
        return jnp.dot(one_hot, source_table, preferred_element_type=jnp.float32).astype(
            jnp.bfloat16
        )

    picked = lax.map(pick_block, grouped)
    return picked.reshape(row_total, source_table.shape[1])


def owner_add(indices, gradients, entity_count):
    start_value = jnp.zeros((entity_count, gradients.shape[1]), jnp.float32)
    return start_value.at[indices].add(gradients)


def local(
    entity_rows,
    request_rows,
    edge_heads,
    edge_rels,
    edge_tails,
    edge_counts,
    negative_rows,
    relation_blocks,
):
    entity_count, feature_width = entity_rows.shape
    part_count = request_rows.shape[1]
    slot_count = request_rows.shape[2]
    r_count, block_count, block_width = (
        relation_blocks.shape[0],
        relation_blocks.shape[1],
        relation_blocks.shape[2],
    )
    neg_count = negative_rows.shape[0]
    owner_lists = lax.all_to_all(request_rows, "ent", split_axis=1, concat_axis=0, tiled=True)
    wanted = pick_rows(owner_lists.reshape(-1), entity_rows).reshape(
        part_count, 1, slot_count, feature_width
    )
    fetched = lax.all_to_all(wanted, "ent", split_axis=0, concat_axis=1, tiled=True)
    fetched = fetched.reshape(part_count * slot_count, feature_width)
    neg_rows = pick_rows(negative_rows, entity_rows)
    edge_dev = edge_heads.shape[0]
    block_size = math.gcd(edge_dev, 256)
    block_total = edge_dev // block_size
    live_count = edge_counts[0]
    positions = jnp.arange(edge_dev, dtype=jnp.int32).reshape(block_total, block_size)
    entity_columns = jnp.arange(entity_count, dtype=jnp.int32)
    slot_columns = jnp.arange(part_count * slot_count, dtype=jnp.int32)
    rel_columns = jnp.arange(r_count, dtype=jnp.int32)
    contract_rows = (((0,), (0,)), ((), ()))

    def edge_block(running, block_inputs):
        slot_acc, entity_acc, neg_acc, relation_acc = running
        head_ids, rel_ids, tail_ids, places = block_inputs
        live_mask = (places < live_count).astype(jnp.float32)
        head_hot = (head_ids[:, None] == entity_columns[None, :]).astype(jnp.bfloat16)
        tail_hot = (tail_ids[:, None] == slot_columns[None, :]).astype(jnp.bfloat16)
        head_rows = jnp.dot(head_hot, entity_rows, preferred_element_type=jnp.float32).astype(
            jnp.bfloat16
        )
        tail_rows = jnp.dot(tail_hot, fetched, preferred_element_type=jnp.float32).astype(
            jnp.bfloat16
        )
        rel_hot = (rel_ids[:, None] == rel_columns[None, :]).astype(jnp.float32)
        head_split = head_rows.reshape(block_size, block_count, block_width)
        proj_all = jnp.einsum(
            "enb,rnbc->renc", head_split, relation_blocks, preferred_element_type=jnp.float32
        )
        projected = (
            jnp.sum(rel_hot.T[:, :, None, None] * proj_all, 0)
            .reshape(block_size, feature_width)
            .astype(jnp.bfloat16)
        )
        projected_wide = projected.astype(jnp.float32)
        positive = jnp.sum(projected_wide * tail_rows.astype(jnp.float32), -1)
        negative = lax.dot_general(
            projected, neg_rows, (((1,), (1,)), ((), ())), preferred_element_type=jnp.float32
        )
        pos_weight = -live_mask * jax.nn.sigmoid(-positive)
        neg_weight = (live_mask[:, None] * jax.nn.sigmoid(negative) / neg_count).astype(
            jnp.bfloat16
        )
        grad_proj = (
            pos_weight[:, None] * tail_rows.astype(jnp.float32)
            + jnp.dot(neg_weight, neg_rows, preferred_element_type=jnp.float32)
        ).astype(jnp.bfloat16)
        weighted = (pos_weight[:, None] * projected_wide).astype(jnp.bfloat16)
        grad_split = grad_proj.reshape(block_size, block_count, block_width)
        back_all = jnp.einsum(
            "enc,rnbc->renb", grad_split, relation_blocks, preferred_element_type=jnp.float32
        )
        head_grad = (
            jnp.sum(rel_hot.T[:, :, None, None] * back_all, 0)
            .reshape(block_size, feature_width)
            .astype(jnp.bfloat16)
        )
        slot_acc = slot_acc + lax.dot_general(
            tail_hot, weighted, contract_rows, preferred_element_type=jnp.float32
        )
        entity_acc = entity_acc + lax.dot_general(
            head_hot, head_grad, contract_rows, preferred_element_type=jnp.float32
        )
        neg_acc = neg_acc + lax.dot_general(
            neg_weight, projected, contract_rows, preferred_element_type=jnp.float32
        )
        masked_heads = rel_hot.T.astype(jnp.bfloat16)[:, :, None, None] * head_split[None]
        relation_acc = relation_acc + jnp.einsum(
            "renb,enc->rnbc", masked_heads, grad_split, preferred_element_type=jnp.float32
        )
        return ((slot_acc, entity_acc, neg_acc, relation_acc), None)

    start_values = (
        jnp.zeros((part_count * slot_count, feature_width), jnp.float32),
        jnp.zeros((entity_count, feature_width), jnp.float32),
        jnp.zeros((neg_count, feature_width), jnp.float32),
        jnp.zeros(relation_blocks.shape, jnp.float32),
    )
    block_inputs = (
        edge_heads.reshape(block_total, block_size),
        edge_rels.reshape(block_total, block_size),
        edge_tails.reshape(block_total, block_size),
        positions,
    )
    (slot_acc, entity_acc, neg_acc, relation_acc), _ = lax.scan(
        edge_block, start_values, block_inputs
    )
    neg_hot = (negative_rows[:, None] == entity_columns[None, :]).astype(jnp.bfloat16)
    entity_acc = entity_acc + lax.dot_general(
        neg_hot, neg_acc.astype(jnp.bfloat16), contract_rows, preferred_element_type=jnp.float32
    )
    slot_grads = slot_acc.reshape(1, part_count, slot_count, feature_width)
    returned = lax.all_to_all(
        slot_grads.astype(jnp.bfloat16), "ent", split_axis=1, concat_axis=0, tiled=True
    ).astype(slot_grads.dtype)
    entity_acc = entity_acc + owner_add(
        owner_lists.reshape(-1), returned.reshape(-1, feature_width), entity_count
    )
    entity_grad = lax.psum(entity_acc, "rel")
    relation_grad = lax.psum(relation_acc, "ent")
    return (entity_grad, relation_grad)


def solution(mesh):
    in_specs = (
        P("ent", None),
        P("ent", None, None),
        P(("ent", "rel")),
        P(("ent", "rel")),
        P(("ent", "rel")),
        P(("ent", "rel")),
        P(("ent", "rel")),
        P("rel", None, None, None),
    )
    out_specs = (P("ent", None), P("rel", None, None, None))
    return jax.shard_map(local, mesh=mesh, in_specs=in_specs, out_specs=out_specs, check_vma=False)
```

profile of v0, /device:TPU:8, one launch (start us, length us, event | category | flops | bytes accessed | tf_op | source)
XLA Modules:
  0.0 383.0 jit_solution(16212449031649504692)
XLA Ops:
  8.6 12.1 %all-to-all-start = ((s32[1,64,32]{2,0,1:T(1,128)}), s32[1,64,32]{2,0,1:T(1,128)S(1)}, u32[]{:S(2)}, u32[]{:S(2)}) async-start(s32[1,64,32]{2,0,1:T(1,128)} %copy.20), calls=%async_computation | async-start | bytes 65536 | tf_op jit(solution)/shard_map/all_to_all | solution.py:48
  20.7 8.5 %all-to-all-done = s32[1,64,32]{2,0,1:T(1,128)S(1)} async-done(((s32[1,64,32]{2,0,1:T(1,128)}), s32[1,64,32]{2,0,1:T(1,128)S(1)}, u32[]{:S(2)}, u32[]{:S(2)}) %all-to-all-start) | async-done | bytes 8224 | tf_op jit(solution)/shard_map/all_to_all | solution.py:48
  30.6 16.5 %while.32 = (s32[]{:T(128)}, bf16[8,256,256]{2,1,0:T(8,128)(2,1)}, s32[8,256]{1,0:T(8,128)S(1)}, bf16[1024,256]{1,0:T(8,128)(2,1)}, s32[]{:T(128)}) while((s32[]{:T(128)}, bf16[8,256,256]{2,1,0:T(8,128)(2,1)}, s32[8,256]{1,0:T(8,128)S(1)}, bf16[1024,256]{1,0:T(8,128)(2,1)}, s32[]{:T(128)}) %tuple.56), condition=%wide.region_1.2_spmd.clone, body=%wide.region_0.1_spmd.clone.sunk | while | flops 134545408 | bytes 658509 | solution.py:20
  30.6 2.1 fusion.90
  32.6 2.0 fusion.90
  34.7 2.0 fusion.90
  36.8 2.1 fusion.90
  38.8 2.1 fusion.90
  40.9 2.0 fusion.90
  42.9 2.0 fusion.90
  45.0 2.1 fusion.90
  47.0 6.5 %all-to-all-start.1 = ((bf16[64,1,32,256]{3,2,1,0:T(8,128)(2,1)}), bf16[64,1,32,256]{3,2,1,0:T(8,128)(2,1)}, u32[]{:S(2)}, u32[]{:S(2)}) async-start(bf16[64,1,32,256]{3,2,1,0:T(8,128)(2,1)} %bitcast.1), calls=%async_computation.1 | async-start | bytes 2097152 | tf_op jit(solution)/shard_map/all_to_all | solution.py:52
  56.9 25.4 %all-to-all-done.1 = bf16[64,1,32,256]{3,2,1,0:T(8,128)(2,1)} async-done(((bf16[64,1,32,256]{3,2,1,0:T(8,128)(2,1)}), bf16[64,1,32,256]{3,2,1,0:T(8,128)(2,1)}, u32[]{:S(2)}, u32[]{:S(2)}) %all-to-all-start.1) | async-done | bytes 1048608 | tf_op jit(solution)/shard_map/all_to_all | solution.py:52
  82.3 38.9 %while.33 = (s32[]{:T(128)}, f32[2048,256]{1,0:T(8,128)S(1)}, f32[1024,256]{1,0:T(8,128)S(1)}, f32[256,256]{1,0:T(8,128)S(1)}, f32[8,8,32,32]{2,3,0,1:T(8,128)},...) while((s32[]{:T(128)}, f32[2048,256]{1,0:T(8,128)S(1)}, ...), condition=%wide.region_6.7_spmd.clone, body=%wide.region_2.6_spmd.clone.sunk | while | flops 1016077568 | bytes 14733582 | solution.py:137
  86.6 2.1 fusion.111
  96.4 2.1 fusion.111
  106.1 2.1 fusion.111
  115.8 2.1 fusion.111
  122.3 5.9 %all-to-all-start.2 = ((bf16[1,64,32,256]{3,2,0,1:T(8,128)(2,1)}), bf16[1,64,32,256]{3,2,0,1:T(8,128)(2,1)S(1)}, u32[]{:S(2)}, u32[]{:S(2)}) async-start(bf16[1,64,32,256]{3,2,0,1:T(8,128)(2,1)} %bitcast.124), calls=%async_computation.2 | async-start | bytes 2097152 | tf_op jit(solution)/shard_map/all_to_all | solution.py:145
  130.4 27.4 %all-to-all-done.2 = bf16[1,64,32,256]{3,2,0,1:T(8,128)(2,1)S(1)} async-done(((bf16[1,64,32,256]{3,2,0,1:T(8,128)(2,1)}), bf16[1,64,32,256]{3,2,0,1:T(8,128)(2,1)S(1)}, u32[]{:S(2)}, u32[]{:S(2)}) %all-to-all-start.2) | async-done | bytes 1048608 | tf_op jit(solution)/shard_map/all_to_all | solution.py:145
  157.7 12.0 %scatter_custom_fusion = f32[1024,256]{1,0:T(8,128)S(1)} fusion(f32[1024,256]{1,0:T(8,128)S(1)} %convolution_add_fusion.4, s32[2048]{0:T(1024)S(1)} %bitcast.138, bf16[2048,256]{1,0:T(8,128)(2,1)S(1)} %bitcast.125), kind=kCustom, calls=%fused_computation.57 | custom fusion | flops 1048576 | bytes 2097152 | tf_op jit(solution)/shard_map/scatter-add | solution.py:26
  170.8 150.9 %all-reduce.5.cloned.1.call-done = f32[8,8,32,32]{3,2,1,0:T(8,128)} async-done(((f32[8,8,32,32]{3,2,1,0:T(8,128)}), f32[8,8,32,32]{3,2,1,0:T(8,128)}) %all-reduce.5.cloned.1.call-update) | async-done | bytes 262160 | tf_op jit(solution)/shard_map/psum | solution.py:152
  321.6 51.3 %all-reduce.3.cloned.1.call-done = f32[1024,256]{1,0:T(8,128)} async-done(((f32[1024,256]{1,0:T(8,128)}), f32[1024,256]{1,0:T(8,128)}) %all-reduce.3.cloned.1.call-update) | async-done | bytes 1048592 | tf_op jit(solution)/shard_map/psum | solution.py:151
  372.9 2.3 copy.51
  (131 shorter events, 41.3 us)
Async XLA Ops:
  8.6 20.7 %all-to-all-start = ((s32[1,64,32]{2,0,1:T(1,128)}), s32[1,64,32]{2,0,1:T(1,128)S(1)}, u32[]{:S(2)}, u32[]{:S(2)}) async-start(s32[1,64,32]{2,0,1:T(1,128)} %copy.20), calls=%async_computation | async-start | bytes 65536 | tf_op jit(solution)/shard_map/all_to_all | solution.py:48
  47.0 6.5 %copy-start.8 = (s32[1024]{0:T(1024)S(1)}, s32[1024]{0:T(1024)}, u32[]{:S(2)}) copy-start(s32[1024]{0:T(1024)} %param.14) | copy-start | bytes 12292
  47.0 6.5 %copy-start.9 = (s32[1024]{0:T(1024)S(1)}, s32[1024]{0:T(1024)}, u32[]{:S(2)}) copy-start(s32[1024]{0:T(1024)} %param.15) | copy-start | bytes 12292
  47.0 6.6 %copy-start.10 = (s32[1024]{0:T(1024)S(1)}, s32[1024]{0:T(1024)}, u32[]{:S(2)}) copy-start(s32[1024]{0:T(1024)} %param.16) | copy-start | bytes 12292
  47.0 35.3 %all-to-all-start.1 = ((bf16[64,1,32,256]{3,2,1,0:T(8,128)(2,1)}), bf16[64,1,32,256]{3,2,1,0:T(8,128)(2,1)}, u32[]{:S(2)}, u32[]{:S(2)}) async-start(bf16[64,1,32,256]{3,2,1,0:T(8,128)(2,1)} %bitcast.1), calls=%async_computation.1 | async-start | bytes 2097152 | tf_op jit(solution)/shard_map/all_to_all | solution.py:52
  86.4 2.6 copy-start.5
  86.6 2.8 copy-start
  90.4 1.7 copy-start.1
  96.1 2.6 copy-start.5
  96.4 2.8 copy-start
  100.1 1.7 copy-start.1
  105.8 2.6 copy-start.5
  106.1 2.8 copy-start
  109.8 1.7 copy-start.1
  115.6 2.6 copy-start.5
  115.8 2.8 copy-start
  119.6 1.7 copy-start.1
  121.2 7.0 %copy-start.7 = (s32[1,64,32]{2,0,1:T(1,128)S(1)}, s32[1,64,32]{2,0,1:T(1,128)}, u32[]{:S(2)}) copy-start(s32[1,64,32]{2,0,1:T(1,128)} %copy-done.6) | copy-start | bytes 24580
  122.3 6.0 %copy-start.2 = (f32[8,8,32,32]{2,3,0,1:T(8,128)S(1)}, f32[8,8,32,32]{2,3,0,1:T(8,128)}, u32[]{:S(2)}) copy-start(f32[8,8,32,32]{2,3,0,1:T(8,128)} %get-tuple-element.138) | copy-start | bytes 786436
  122.3 35.4 %all-to-all-start.2 = ((bf16[1,64,32,256]{3,2,0,1:T(8,128)(2,1)}), bf16[1,64,32,256]{3,2,0,1:T(8,128)(2,1)S(1)}, u32[]{:S(2)}, u32[]{:S(2)}) async-start(bf16[1,64,32,256]{3,2,0,1:T(8,128)(2,1)} %bitcast.124), calls=%async_computation.2 | async-start | bytes 2097152 | tf_op jit(solution)/shard_map/all_to_all | solution.py:145
  128.2 1.6 copy-start.11
  128.2 193.4 %all-reduce.5.cloned.1.call-start = ((), (), s32[]{:S(2)}) async-start(), calls=%async_computation.4 | async-start | bytes 2097152 | tf_op jit(solution)/shard_map/psum | solution.py:152
  129.8 243.2 %all-reduce.3.cloned.1.call-start = ((), (), s32[]{:S(2)}) async-start(), calls=%async_computation.3 | async-start | bytes 2097152 | tf_op jit(solution)/shard_map/psum | solution.py:151
  321.6 53.6 %copy-start.4 = (f32[8,8,32,32]{3,2,1,0:T(8,128)S(1)}, f32[8,8,32,32]{3,2,1,0:T(8,128)}, u32[]{:S(2)}) copy-start(f32[8,8,32,32]{3,2,1,0:T(8,128)} %all-reduce.5.cloned.1.call-done) | copy-start | bytes 786436
  (2 other events, 2.3 us)
Sparse Core Ops, SparseCore 0:
  132.4 189.1 all-reduce.4
  324.6 48.3 all-reduce.2
where the time goes:
time: 384 us; the launch traced here: 383 us
  waiting for transfers between devices  263 us (68%)
  matrix products  53.8 us (14%)
  starting transfers between devices  24.5 us (6%)
  other arithmetic  16.5 us (4%)
  between operations  14.2 us (4%)
  local copies, waits for them, and re-layouts  9.81 us (3%)
    psum x1, waiting for transfers between devices, local(): relation_grad = lax.psum(relation_acc, 'ent')  151 us
    psum x1, waiting for transfers between devices, local(): entity_grad = lax.psum(entity_acc, 'rel')  51.3 us
    all_to_all x1, waiting for transfers between devices, local(): lax.all_to_all(slot_grads.astype(jnp.bfloat16), 'ent', split_axis=1, conc...  27.4 us
    all_to_all x1, waiting for transfers between devices, local(): lax.all_to_all(wanted, 'ent', split_axis=0, concat_axis=1, tiled=True)  25.4 us
    dot_general x9, matrix products, pick_block(): jnp.dot(one_hot, source_table, preferred_element_type=jnp.float32)  17.8 us
    all_to_all x1, starting transfers between devices, local(): lax.all_to_all(request_rows, 'ent', split_axis=1, concat_axis=0, tiled=True)  12.1 us
    scatter-add x1, other arithmetic, owner_add(): return start_value.at[indices].add(gradients)  12 us
    all_to_all x1, waiting for transfers between devices, local(): lax.all_to_all(request_rows, 'ent', split_axis=1, concat_axis=0, tiled=True)  8.54 us
  transfers between devices with their start and end apart: 5, of which 5 were waited for; matrix products, arithmetic and copies ran while one was open for 5% of the time, Pallas kernels for 0%

commit v1 on v0

--- a/solution.py
+++ b/solution.py
@@ -148,7 +148,8 @@
     entity_acc = entity_acc + owner_add(
         owner_lists.reshape(-1), returned.reshape(-1, feature_width), entity_count
     )
-    entity_grad = lax.psum(entity_acc, "rel")
+    shards = lax.all_gather(entity_acc, "rel")
+    entity_grad = jnp.sum(shards, axis=0)
     relation_grad = lax.psum(relation_acc, "ent")
     return (entity_grad, relation_grad)
 

time: 384 us -> 371 us (0.966)
  waiting for transfers between devices: 263 us -> 246 us
    psum x1 -> x0, waiting for transfers between devices: 51.3 us -> none  [local(): entity_grad = lax.psum(entity_acc, 'rel')]
    all_gather x0 -> x1, waiting for transfers between devices: none -> 45.9 us  [local(): shards = lax.all_gather(entity_acc, 'rel')]
    psum x1, waiting for transfers between devices: 151 us -> 138 us  [local(): relation_grad = lax.psum(relation_acc, 'ent')]
  transfers between devices with their start and end apart: 5 -> 5, of which waited for: 5 -> 5; matrix products, arithmetic and copies ran while one was open for 5% -> 2% of each run, Pallas kernels for 0% -> 0%
where the time goes in v1:
time: 371 us; the launch traced here: 369 us
  waiting for transfers between devices  246 us (66%)
  matrix products  53.8 us (15%)
  starting transfers between devices  24.4 us (7%)
  other arithmetic  20.1 us (5%)
  between operations  15.7 us (4%)
  local copies, waits for them, and re-layouts  8.78 us (2%)
    psum x1, waiting for transfers between devices, local(): relation_grad = lax.psum(relation_acc, 'ent')  138 us
    all_gather x1, waiting for transfers between devices, local(): shards = lax.all_gather(entity_acc, 'rel')  45.9 us
    all_to_all x1, waiting for transfers between devices, local(): lax.all_to_all(slot_grads.astype(jnp.bfloat16), 'ent', split_axis=1, conc...  28 us
    all_to_all x1, waiting for transfers between devices, local(): lax.all_to_all(wanted, 'ent', split_axis=0, concat_axis=1, tiled=True)  25.4 us
    dot_general x9, matrix products, pick_block(): jnp.dot(one_hot, source_table, preferred_element_type=jnp.float32)  17.8 us
    all_to_all x1, starting transfers between devices, local(): lax.all_to_all(request_rows, 'ent', split_axis=1, concat_axis=0, tiled=True)  12.1 us
    scatter-add x1, other arithmetic, owner_add(): return start_value.at[indices].add(gradients)  12 us
    all_to_all x1, waiting for transfers between devices, local(): lax.all_to_all(request_rows, 'ent', split_axis=1, concat_axis=0, tiled=True)  8.54 us
  transfers between devices with their start and end apart: 5, of which 5 were waited for; matrix products, arithmetic and copies ran while one was open for 2% of the time, Pallas kernels for 0%

profile of v1, /device:TPU:8, one launch (start us, length us, event | category | flops | bytes accessed | tf_op | source)
XLA Modules:
  0.0 369.3 jit_solution(6209630855340743027)
XLA Ops:
  9.4 12.1 %all-to-all-start = ((s32[1,64,32]{2,0,1:T(1,128)}), s32[1,64,32]{2,0,1:T(1,128)S(1)}, u32[]{:S(2)}, u32[]{:S(2)}) async-start(s32[1,64,32]{2,0,1:T(1,128)} %copy.20), calls=%async_computation | async-start | bytes 65536 | tf_op jit(solution)/shard_map/all_to_all | solution.py:48
  21.5 8.5 %all-to-all-done = s32[1,64,32]{2,0,1:T(1,128)S(1)} async-done(((s32[1,64,32]{2,0,1:T(1,128)}), s32[1,64,32]{2,0,1:T(1,128)S(1)}, u32[]{:S(2)}, u32[]{:S(2)}) %all-to-all-start) | async-done | bytes 8224 | tf_op jit(solution)/shard_map/all_to_all | solution.py:48
  31.4 16.5 %while.32 = (s32[]{:T(128)}, bf16[8,256,256]{2,1,0:T(8,128)(2,1)}, s32[8,256]{1,0:T(8,128)S(1)}, bf16[1024,256]{1,0:T(8,128)(2,1)}, s32[]{:T(128)}) while((s32[]{:T(128)}, bf16[8,256,256]{2,1,0:T(8,128)(2,1)}, s32[8,256]{1,0:T(8,128)S(1)}, bf16[1024,256]{1,0:T(8,128)(2,1)}, s32[]{:T(128)}) %tuple.56), condition=%wide.region_1.2_spmd.clone, body=%wide.region_0.1_spmd.clone.sunk | while | flops 134545408 | bytes 658509 | solution.py:20
  31.4 2.1 fusion.90
  33.5 2.0 fusion.90
  35.5 2.1 fusion.90
  37.6 2.1 fusion.90
  39.6 2.1 fusion.90
  41.7 2.0 fusion.90
  45.8 2.1 fusion.90
  47.9 6.5 %all-to-all-start.1 = ((bf16[64,1,32,256]{3,2,1,0:T(8,128)(2,1)}), bf16[64,1,32,256]{3,2,1,0:T(8,128)(2,1)}, u32[]{:S(2)}, u32[]{:S(2)}) async-start(bf16[64,1,32,256]{3,2,1,0:T(8,128)(2,1)} %bitcast.1), calls=%async_computation.1 | async-start | bytes 2097152 | tf_op jit(solution)/shard_map/all_to_all | solution.py:52
  57.8 25.4 %all-to-all-done.1 = bf16[64,1,32,256]{3,2,1,0:T(8,128)(2,1)} async-done(((bf16[64,1,32,256]{3,2,1,0:T(8,128)(2,1)}), bf16[64,1,32,256]{3,2,1,0:T(8,128)(2,1)}, u32[]{:S(2)}, u32[]{:S(2)}) %all-to-all-start.1) | async-done | bytes 1048608 | tf_op jit(solution)/shard_map/all_to_all | solution.py:52
  83.1 38.9 %while.33 = (s32[]{:T(128)}, f32[2048,256]{1,0:T(8,128)S(1)}, f32[1024,256]{1,0:T(8,128)S(1)}, f32[256,256]{1,0:T(8,128)S(1)}, f32[8,8,32,32]{2,3,0,1:T(8,128)},...) while((s32[]{:T(128)}, f32[2048,256]{1,0:T(8,128)S(1)}, ...), condition=%wide.region_6.7_spmd.clone, body=%wide.region_2.6_spmd.clone.sunk | while | flops 1016077568 | bytes 14733582 | solution.py:137
  87.5 2.1 fusion.111
  97.2 2.1 fusion.111
  106.9 2.1 fusion.111
  116.7 2.1 fusion.111
  123.2 5.7 %all-to-all-start.2 = ((bf16[1,64,32,256]{3,2,0,1:T(8,128)(2,1)}), bf16[1,64,32,256]{3,2,0,1:T(8,128)(2,1)S(1)}, u32[]{:S(2)}, u32[]{:S(2)}) async-start(bf16[1,64,32,256]{3,2,0,1:T(8,128)(2,1)} %bitcast.125), calls=%async_computation.2 | async-start | bytes 2097152 | tf_op jit(solution)/shard_map/all_to_all | solution.py:145
  129.7 28.0 %all-to-all-done.2 = bf16[1,64,32,256]{3,2,0,1:T(8,128)(2,1)S(1)} async-done(((bf16[1,64,32,256]{3,2,0,1:T(8,128)(2,1)}), bf16[1,64,32,256]{3,2,0,1:T(8,128)(2,1)S(1)}, u32[]{:S(2)}, u32[]{:S(2)}) %all-to-all-start.2) | async-done | bytes 1048608 | tf_op jit(solution)/shard_map/all_to_all | solution.py:145
  157.7 12.0 %scatter_custom_fusion = f32[1024,256]{1,0:T(8,128)S(1)} fusion(f32[1024,256]{1,0:T(8,128)S(1)} %convolution_add_fusion.4, s32[2048]{0:T(1024)S(1)} %bitcast.140, bf16[2048,256]{1,0:T(8,128)(2,1)S(1)} %bitcast.127), kind=kCustom, calls=%fused_computation.57 | custom fusion | flops 1048576 | bytes 2097152 | tf_op jit(solution)/shard_map/scatter-add | solution.py:26
  172.1 45.9 %all-gather.3.cloned.1.call-done = f32[4096,256]{1,0:T(8,128)} async-done(((f32[1024,256]{1,0:T(8,128)}), f32[4096,256]{1,0:T(8,128)}) %all-gather.3.cloned.1.call-update) | async-done | bytes 4194320 | tf_op jit(solution)/shard_map/all_gather | solution.py:151
  218.0 3.6 reduce_sum.36
  221.6 137.9 %all-reduce.2.cloned.1.call-done = f32[8,8,32,32]{3,2,1,0:T(8,128)} async-done(((f32[8,8,32,32]{3,2,1,0:T(8,128)}), f32[8,8,32,32]{3,2,1,0:T(8,128)}) %all-reduce.2.cloned.1.call-update) | async-done | bytes 262160 | tf_op jit(solution)/shard_map/psum | solution.py:153
  359.6 2.3 copy.50
  (129 shorter events, 42.3 us)
Async XLA Ops:
  9.4 20.7 %all-to-all-start = ((s32[1,64,32]{2,0,1:T(1,128)}), s32[1,64,32]{2,0,1:T(1,128)S(1)}, u32[]{:S(2)}, u32[]{:S(2)}) async-start(s32[1,64,32]{2,0,1:T(1,128)} %copy.20), calls=%async_computation | async-start | bytes 65536 | tf_op jit(solution)/shard_map/all_to_all | solution.py:48
  30.1 1.3 copy-start.5
  47.9 6.5 %copy-start.7 = (s32[1024]{0:T(1024)S(1)}, s32[1024]{0:T(1024)}, u32[]{:S(2)}) copy-start(s32[1024]{0:T(1024)} %param.14) | copy-start | bytes 12292
  47.9 6.5 %copy-start.8 = (s32[1024]{0:T(1024)S(1)}, s32[1024]{0:T(1024)}, u32[]{:S(2)}) copy-start(s32[1024]{0:T(1024)} %param.15) | copy-start | bytes 12292
  47.9 6.6 %copy-start.9 = (s32[1024]{0:T(1024)S(1)}, s32[1024]{0:T(1024)}, u32[]{:S(2)}) copy-start(s32[1024]{0:T(1024)} %param.16) | copy-start | bytes 12292
  47.9 35.3 %all-to-all-start.1 = ((bf16[64,1,32,256]{3,2,1,0:T(8,128)(2,1)}), bf16[64,1,32,256]{3,2,1,0:T(8,128)(2,1)}, u32[]{:S(2)}, u32[]{:S(2)}) async-start(bf16[64,1,32,256]{3,2,1,0:T(8,128)(2,1)} %bitcast.1), calls=%async_computation.1 | async-start | bytes 2097152 | tf_op jit(solution)/shard_map/all_to_all | solution.py:52
  87.2 2.6 copy-start.4
  87.5 2.8 copy-start
  91.2 1.7 copy-start.1
  96.9 2.6 copy-start.4
  97.2 2.8 copy-start
  100.9 1.7 copy-start.1
  106.7 2.6 copy-start.4
  106.9 2.8 copy-start
  110.7 1.7 copy-start.1
  116.4 2.6 copy-start.4
  116.7 2.8 copy-start
  120.4 1.7 copy-start.1
  122.1 6.9 %copy-start.6 = (s32[1,64,32]{2,0,1:T(1,128)S(1)}, s32[1,64,32]{2,0,1:T(1,128)}, u32[]{:S(2)}) copy-start(s32[1,64,32]{2,0,1:T(1,128)} %copy-done.5) | copy-start | bytes 24580
  122.1 7.0 %copy-start.10 = (s32[256]{0:T(256)S(1)}, s32[256]{0:T(256)}, u32[]{:S(2)}) copy-start(s32[256]{0:T(256)} %param.18) | copy-start | bytes 3076
  123.2 34.5 %all-to-all-start.2 = ((bf16[1,64,32,256]{3,2,0,1:T(8,128)(2,1)}), bf16[1,64,32,256]{3,2,0,1:T(8,128)(2,1)S(1)}, u32[]{:S(2)}, u32[]{:S(2)}) async-start(bf16[1,64,32,256]{3,2,0,1:T(8,128)(2,1)} %bitcast.125), calls=%async_computation.2 | async-start | bytes 2097152 | tf_op jit(solution)/shard_map/all_to_all | solution.py:145
  128.9 89.1 %all-gather.3.cloned.1.call-start = ((), (), s32[]{:S(2)}) async-start(), calls=%async_computation.4 | async-start | bytes 5242880 | tf_op jit(solution)/shard_map/all_gather | solution.py:151
  129.6 41.1 %copy-start.2 = (f32[8,8,32,32]{2,3,0,1:T(8,128)S(1)}, f32[8,8,32,32]{2,3,0,1:T(8,128)}, u32[]{:S(2)}) copy-start(f32[8,8,32,32]{2,3,0,1:T(8,128)} %get-tuple-element.138) | copy-start | bytes 786436
  170.7 188.9 %all-reduce.2.cloned.1.call-start = ((), (), s32[]{:S(2)}) async-start(), calls=%async_computation.3 | async-start | bytes 2097152 | tf_op jit(solution)/shard_map/psum | solution.py:153
  (1 other events, 1.0 us)
Sparse Core Ops, SparseCore 0:
  170.8 47.1 all-gather.2
Sparse Core Ops, SparseCore 1:
  175.2 184.3 all-reduce.1
